TPU v7x, 512 devices: a whole 4x4x16 slice. The times are simulated.
512 devices in a mesh: row: 32 (over z, x_hi), col: 16 (over x_lo, y, core).
Axes of the slice: x: 4 (x_hi: 2, x_lo: 2; x = x_hi * 2 + x_lo), y: 4, z: 16, core: 2. Of those that a mesh axis runs over, the one named last changes fastest.
Arguments:
- inverse_set: float32 [1, 32, 128, 2, 16, 128], P(None, 'row', None, None, 'col'), may hold values from -6 to 6
- presence: int32 [1, 32, 2, 16], P(None, 'row', None, 'col'), may hold values 0 or 1
- factor: float32 [1, 32, 128, 512], P(None, 'row'), may hold values from -0.09375 to 0.09375
- dinv: float32 [512, 512], P('row', 'col'), may hold values from -6 to 6
Outputs:
- off_diag: float32 [1, 32, 128, 512], P(None, 'row', 'col')
- diag_block: float32 [512, 512], P('row', 'col')
All inputs are finite; a program needn't handle non-finite values. No bound on the sum of `presence` on one device may be relied on, other than what follows from the above.
Results may differ from a plain program's by a relative error of at most 0.00007.
Values sent between devices are 32-bit elements; how exact they have to be, the bound alone decides.
A program may use at most 64 MiB of HBM per device.

v0:
```python
import jax
import jax.numpy as jnp
from jax import lax
from jax.sharding import PartitionSpec as P


def spread(value, axis, root):
    mine = lax.axis_index(axis) == root
    return lax.psum(jnp.where(mine, value, jnp.zeros_like(value)), axis)


def local(inverse_set, presence, factor, dinv):
    groups_row = lax.axis_size("row")
    groups_col = lax.axis_size("col")
    group_ratio = groups_row // groups_col
    col_index = lax.axis_index("col")
    block_order = factor.shape[2]
    width = factor.shape[3]
    block_cols = inverse_set.shape[3]
    own_rows = factor[:, 0]
    masked = (
        inverse_set[:, 0, :, :, 0, :] * presence[:, 0, :, 0].astype(jnp.float32)[:, None, :, None]
    )
    pieces = []
    for level in range(group_ratio):
        pieces.append(spread(own_rows, "row", level * groups_col + col_index))
    columns = jnp.stack(pieces, axis=1).reshape(block_cols, block_order, width)
    partial_value = jnp.einsum("axbz,bzy->axy", masked, columns, precision=lax.Precision.HIGHEST)
    update = lax.psum_scatter(partial_value, "col", scatter_dimension=1, tiled=True)
    share = block_order // groups_col
    rows_mine = lax.dynamic_slice_in_dim(own_rows, col_index * share, share, 1)
    diag_part = jnp.einsum("axy,axw->yw", rows_mine, update, precision=lax.Precision.HIGHEST)
    diag_half = lax.psum_scatter(diag_part, "col", scatter_dimension=1, tiled=True)
    diag_sum = lax.psum_scatter(diag_half, "row", scatter_dimension=0, tiled=True)
    off_diag = (-update)[:, None, :, :]
    diag_block = dinv + diag_sum
    return (off_diag, diag_block)


def solution(mesh):
    in_specs = (
        P(None, "row", None, None, "col", None),
        P(None, "row", None, "col"),
        P(None, "row", None, None),
        P("row", "col"),
    )
    out_specs = (P(None, "row", "col", None), P("row", "col"))
    return jax.shard_map(local, mesh=mesh, in_specs=in_specs, out_specs=out_specs, check_vma=False)
```

profile of v0, /device:TPU:1, one launch (start us, length us, event | category | flops | bytes accessed | tf_op | source)
XLA Modules:
  0.0 1106.9 jit_solution(4744221916118201594)
XLA Ops:
  7.2 0.0 all-reduce.3.cloned.1.call-start
  7.2 1.8 broadcast_select_fusion.1
  9.0 0.0 copy-start.3
  9.0 0.0 copy-start
  9.0 0.0 all-reduce.3.cloned.1.call-update
  9.1 0.0 reduce-scatter.6.cloned.1.call-start
  9.1 0.6 copy-done.3
  9.7 0.3 copy-done
  9.9 0.2 broadcast_multiply_fusion
  10.1 295.1 %all-reduce.3.cloned.1.call-done = (f32[1,1,128,512]{3,2,1,0:T(8,128)}, f32[1,1,128,512]{3,2,1,0:T(8,128)}) async-done(((f32[1,1,128,512]{3,2,1,0:T(8,128)}, f32[1,1,128,512]{3,2,1,0:T(8,128)}), (f32[1,1,128,512]{3,2,1,0:T(8,128)}, f32[1,1,128,512]{3,2,1,0:T(8,128)})) %all-reduce.3.cloned.1.call-update) | async-done | bytes 524304 | tf_op jit(solution)/shard_map/psum | solution.py:9
  305.2 2.1 convolution_bitcast_fusion
  307.3 0.0 reduce-scatter.6.cloned.1.call-update
  307.4 0.0 reduce-scatter.8.cloned.1.call-start
  307.4 84.6 %reduce-scatter.6.cloned.1.call-done = f32[1,8,512]{2,1,0:T(8,128)} async-done(((f32[1,128,512]{2,1,0:T(8,128)}), f32[1,8,512]{2,1,0:T(8,128)}) %reduce-scatter.6.cloned.1.call-update) | async-done | bytes 16400 | tf_op jit(solution)/shard_map/reduce_scatter | solution.py:29
  392.0 2.7 fusion.3
  394.7 0.0 copy-start.2
  394.7 0.0 reduce-scatter.8.cloned.1.call-update
  394.8 0.0 reduce-scatter.10.cloned.1.call-start
  394.8 0.6 copy-done.2
  395.4 0.1 copy.10
  395.5 67.8 %reduce-scatter.8.cloned.1.call-done = f32[512,32]{0,1:T(8,128)} async-done(((f32[512,512]{0,1:T(8,128)}), f32[512,32]{0,1:T(8,128)}) %reduce-scatter.8.cloned.1.call-update) | async-done | bytes 65552 | tf_op jit(solution)/shard_map/reduce_scatter | solution.py:33
  463.3 1.7 copy.12
  465.0 0.0 copy-start.1
  465.0 0.0 reduce-scatter.10.cloned.1.call-update
  465.0 0.7 copy-done.1
  465.7 0.6 negate_bitcast_fusion
  466.3 632.6 %reduce-scatter.10.cloned.1.call-done = f32[16,32]{1,0:T(8,128)} async-done(((f32[512,32]{1,0:T(8,128)}), f32[16,32]{1,0:T(8,128)}) %reduce-scatter.10.cloned.1.call-update) | async-done | bytes 2064
  1099.0 0.8 copy.13
  1099.7 0.7 copy.11
  (2 shorter events, 0.0 us)
Async XLA Ops:
  7.2 298.0 %all-reduce.3.cloned.1.call-start = ((), (), s32[]{:S(2)}) async-start(), calls=%async_computation.6 | async-start | bytes 1048576 | tf_op jit(solution)/shard_map/psum | solution.py:9
  9.0 0.7 copy-start.3
  9.0 0.9 copy-start
  9.1 383.0 %reduce-scatter.6.cloned.1.call-start = ((), (), s32[]{:S(2)}) async-start(), calls=%async_computation.3 | async-start | bytes 278528 | tf_op jit(solution)/shard_map/reduce_scatter | solution.py:29
  307.4 156.0 %reduce-scatter.8.cloned.1.call-start = ((), (), s32[]{:S(2)}) async-start(), calls=%async_computation.4 | async-start | bytes 1114112 | tf_op jit(solution)/shard_map/reduce_scatter | solution.py:33
  394.7 0.7 copy-start.2
  394.8 704.2 %reduce-scatter.10.cloned.1.call-start = ((), (), s32[]{:S(2)}) async-start(), calls=%async_computation.5 | async-start | bytes 270336
  465.0 0.7 copy-start.1
Sparse Core Ops, SparseCore 0:
  10.9 294.2 all-reduce.2
  308.0 83.9 reduce-scatter.5
  394.9 68.3 reduce-scatter.7
  467.5 631.3 reduce-scatter.9
where the time goes:
time: 1120 us; the launch traced here: 1110 us
  waiting for transfers between devices  1080 us (96%)
  between operations  13.8 us (1%)
    unnamed x5, waiting for transfers between devices  633 us
    psum x1, waiting for transfers between devices, spread(): return lax.psum(jnp.where(mine, value, jnp.zeros_like(value)), axis)  295 us
    reduce_scatter x1, waiting for transfers between devices, local(): lax.psum_scatter(partial_value, 'col', scatter_dimension=1, tiled=True)  84.6 us
    reduce_scatter x1, waiting for transfers between devices, local(): lax.psum_scatter(diag_part, 'col', scatter_dimension=1, tiled=True)  67.8 us
  transfers between devices with their start and end apart: 4, of which 4 were waited for; matrix products, arithmetic and copies ran while one was open for 0% of the time, Pallas kernels for 0%

commit v1 on v0

v1 whole, which is shorter than its diff:
```python
import jax
import jax.numpy as jnp
from jax import lax
from jax.experimental import pallas as pl
from jax.experimental.pallas import tpu as pltpu
from jax.sharding import PartitionSpec as P

MESH = pl.DeviceIdType.MESH
NROW = 32
NCOL = 16
F32 = jnp.float32
BF16 = jnp.bfloat16
NT = (((1,), (1,)), ((), ()))


def split(value):
    high = value.astype(BF16)
    return high, (value - high.astype(F32)).astype(BF16)


def dot_nt(a, b):
    return lax.dot_general(a, b, NT, preferred_element_type=F32)


def kernel(
    inv_hbm, pres_ref, fac_hbm, off_ref, diag_ref,
    a_raw, f_raw, ft, abuf, fbuf, pad, q, trecv, vbuf, vrecv,
    load_sem, f_send, f_recv, b_recv, a_send, a_recv, core_recv, t_send, t_recv, v_send, v_recv,
):
    r = lax.axis_index("row")
    c = lax.axis_index("col")
    xh = lax.rem(r, 2)
    core = lax.rem(c, 2)
    y = lax.rem(lax.div(c, 2), 4)
    xl = lax.div(c, 8)

    load_f = pltpu.make_async_copy(fac_hbm, f_raw, load_sem.at[0])
    load_a = pltpu.make_async_copy(inv_hbm, a_raw, load_sem.at[1])
    load_f.start()
    load_a.start()

    def other(col):
        return lax.rem(col + 8, NCOL)

    r_pair = r + 1 - 2 * xh
    c_x = other(c)
    c_up = xl * 8 + lax.rem(y + 1, 4) * 2 + core
    c_down = xl * 8 + lax.rem(y + 3, 4) * 2 + core
    c_far = xl * 8 + lax.rem(y + 2, 4) * 2 + core
    c_core = c + 1 - 2 * core

    z_up = (lax.rem(r + 2, NROW), c)
    z_down = (lax.rem(r + 30, NROW), c)
    cross = (r_pair, c_x)
    x_pair = (r, c_x)
    y_up = (r, c_up)
    y_down = (r, c_down)
    twin = (r, c_core)

    barrier = pltpu.get_barrier_semaphore()
    for peer in (z_up, z_down, cross, x_pair, y_up, y_down, twin):
        pl.semaphore_signal(barrier, inc=1, device_id=peer, device_id_type=MESH)

    pad[...] = jnp.zeros_like(pad)

    load_f.wait()
    for part in range(4):
        ft[128 * part : 128 * (part + 1), :] = f_raw[:, 128 * part : 128 * (part + 1)].T
    own_rows = pl.multiple_of(32 * c, 32)
    cross_rows = pl.multiple_of(32 * c_x, 32)
    fbuf[r] = ft[pl.ds(own_rows, 32), :]

    load_a.wait()
    for b in range(2):
        abuf[c, b] = a_raw[pl.ds(b, 128, stride=2), :] * pres_ref[0, b].astype(F32)

    pl.semaphore_wait(barrier, 7)

    def send(src, dst, send_sem, recv_sem, peer):
        pltpu.make_async_remote_copy(
            src_ref=src, dst_ref=dst, send_sem=send_sem, recv_sem=recv_sem,
            device_id=peer, device_id_type=MESH,
        ).start()

    def wait(ref, sem):
        pltpu.make_async_copy(ref, ref, sem).wait()

    bases = (r, r_pair)

    def slot(way, chunk, dist):
        step = -2 * dist if way == 0 else 2 * dist
        return lax.rem(bases[chunk] + step + NROW, NROW)

    def reach(way, chunk):
        return 8 if way == chunk else 7

    def pass_on(way, chunk, dist):
        if dist > reach(way, chunk):
            return
        at = slot(way, chunk, dist - 1)
        src = ft.at[pl.ds(own_rows, 32), :] if dist == 1 and chunk == 0 else fbuf.at[at]
        send(src, fbuf.at[at], f_send, f_recv.at[way, chunk, dist - 1], z_up if way == 0 else z_down)

    def take(way, chunk, dist):
        if dist > reach(way, chunk):
            return
        wait(fbuf.at[slot(way, chunk, dist)], f_recv.at[way, chunk, dist - 1])
        pass_on(way, chunk, dist + 1)

    def give(col, b, peer, sem):
        send(abuf.at[col, b], abuf.at[col, b], a_send, sem, peer)

    def got(col, b, sem):
        wait(abuf.at[col, b], a_recv.at[sem])

    pass_on(0, 0, 1)
    pass_on(1, 0, 1)
    send(ft.at[pl.ds(cross_rows, 32), :], fbuf.at[r], f_send, b_recv, cross)
    for b in range(2):
        give(c, b, y_up, a_recv.at[b])
        give(c, b, y_down, a_recv.at[2 + b])
        give(c, b, x_pair, a_recv.at[4 + b])
        give(c, b, twin, core_recv)

    def near_y(b):
        got(c_down, b, b)
        if b == 0:
            give(c_down, b, y_up, a_recv.at[6])
        give(c_down, b, twin, core_recv)
        got(c_up, b, 2 + b)
        if b == 1:
            give(c_up, b, y_down, a_recv.at[7])
        give(c_up, b, twin, core_recv)

    def near_x(b):
        got(c_x, b, 4 + b)
        give(c_x, b, y_up, a_recv.at[8 + b])
        give(c_x, b, y_down, a_recv.at[10 + b])
        give(c_x, b, twin, core_recv)

    def far_y(b):
        got(c_far, b, 6 + b)
        give(c_far, b, x_pair, a_recv.at[12 + b])
        give(c_far, b, twin, core_recv)

    def diagonal(b):
        got(other(c_down), b, 8 + b)
        give(other(c_down), b, twin, core_recv)
        got(other(c_up), b, 10 + b)
        give(other(c_up), b, twin, core_recv)

    def farthest(b):
        got(other(c_far), b, 12 + b)
        give(other(c_far), b, twin, core_recv)

    def both(chunk, dist):
        take(0, chunk, dist)
        take(1, chunk, dist)

    wait(fbuf.at[r_pair], b_recv)
    pass_on(0, 1, 1)
    pass_on(1, 1, 1)
    both(0, 1)
    near_y(0)
    near_x(0)
    both(1, 1)
    both(0, 2)
    near_y(1)
    near_x(1)
    both(1, 2)
    both(0, 3)
    far_y(0)
    far_y(1)
    both(1, 3)
    both(0, 4)
    diagonal(0)
    both(1, 4)
    both(0, 5)
    diagonal(1)
    both(1, 5)
    both(0, 6)
    farthest(0)
    farthest(1)
    both(1, 6)
    both(0, 7)
    both(1, 7)
    wait(abuf.at[pl.ds(0, 8)], core_recv)

    def block(total, at):
        high, low = split(fbuf[at])
        a_high, a_low = split(abuf[lax.rem(at, NCOL), lax.div(at, NCOL)])
        first = dot_nt(jnp.concatenate([high, low], axis=0), a_high)
        return total + (first[:32] + first[32:]) + dot_nt(high, a_low)

    def near(dist, total):
        for chunk in range(2):
            total = block(total, lax.rem(bases[chunk] + 2 * dist, NROW))
            total = block(total, lax.rem(bases[chunk] - 2 * dist + NROW, NROW))
        return total

    total = jnp.zeros((32, 128), F32)
    for chunk in range(2):
        total = block(total, bases[chunk])
    total = lax.fori_loop(1, 8, near, total)
    for chunk in range(2):
        take(chunk, chunk, 8)
        total = block(total, slot(chunk, chunk, 8))

    t_high, t_low = split(total)
    packed = jnp.zeros((128, 128), F32)
    for g in range(4):
        high, low = split(ft[pl.ds(g, 128, stride=4), :])
        parts = []
        for half in (t_high, t_low):
            zero = jnp.zeros((32, 128), BF16)
            parts.append(jnp.concatenate([half if g == at else zero for at in range(4)], axis=0))
        first = dot_nt(jnp.concatenate([high, low], axis=0), parts[0])
        packed = packed + (first[:128] + first[128:]) + dot_nt(high, parts[1])
    for at in range(NROW):
        q[at] = packed[4 * at : 4 * at + 4, :]
    far_first = sorted(range(1, NROW), key=lambda step: -min(step // 2, 16 - step // 2))
    for step in far_first:
        goal = lax.rem(r + step, NROW)
        send(q.at[goal], trecv.at[step - 1], t_send, t_recv, (goal, c))

    pad[pl.ds(pl.multiple_of(32 * lax.rem(c, 4), 32), 32), :] = total
    vbuf[...] = pad[...].T
    vrecv[c] = vbuf[pl.ds(pl.multiple_of(8 * c, 8), 8), :]
    for step in range(1, NCOL):
        goal = lax.rem(c + step, NCOL)
        send(vbuf.at[pl.ds(pl.multiple_of(8 * goal, 8), 8), :], vrecv.at[c], v_send, v_recv, (r, goal))

    wait(vrecv.at[pl.ds(0, NCOL - 1)], v_recv)
    for g in range(4):
        rows = vrecv[4 * g] + vrecv[4 * g + 1] + vrecv[4 * g + 2] + vrecv[4 * g + 3]
        off_ref[:, 128 * g : 128 * (g + 1)] = rows

    wait(trecv, t_recv)
    tile = q[r]
    for step in range(NROW - 1):
        tile = tile + trecv[step]
    for g in range(4):
        diag_ref[pl.ds(g, 4, stride=4), :] = tile[:, 32 * g : 32 * (g + 1)]

    wait(fbuf.at[pl.ds(0, 31)], f_send)
    wait(abuf.at[pl.ds(0, 15)], a_send)
    wait(q.at[pl.ds(0, 31)], t_send)
    wait(vrecv.at[pl.ds(0, NCOL - 1)], v_send)


def local(inverse_set, presence, factor, dinv):
    update, diag_sum = pl.pallas_call(
        kernel,
        out_shape=(jax.ShapeDtypeStruct((8, 512), F32), jax.ShapeDtypeStruct((16, 32), F32)),
        in_specs=[
            pl.BlockSpec(memory_space=pl.ANY),
            pl.BlockSpec(memory_space=pltpu.SMEM),
            pl.BlockSpec(memory_space=pl.ANY),
        ],
        out_specs=(pl.BlockSpec(memory_space=pltpu.VMEM), pl.BlockSpec(memory_space=pltpu.VMEM)),
        scratch_shapes=[
            pltpu.VMEM((256, 128), F32),
            pltpu.VMEM((128, 512), F32),
            pltpu.VMEM((512, 128), F32),
            pltpu.VMEM((NCOL, 2, 128, 128), F32),
            pltpu.VMEM((NROW, 32, 128), F32),
            pltpu.VMEM((128, 128), F32),
            pltpu.VMEM((NROW, 4, 128), F32),
            pltpu.VMEM((NROW - 1, 4, 128), F32),
            pltpu.VMEM((128, 128), F32),
            pltpu.VMEM((NCOL, 8, 128), F32),
            pltpu.SemaphoreType.DMA((2,)),
            pltpu.SemaphoreType.DMA,
            pltpu.SemaphoreType.DMA((2, 2, 8)),
            pltpu.SemaphoreType.DMA,
            pltpu.SemaphoreType.DMA,
            pltpu.SemaphoreType.DMA((14,)),
            pltpu.SemaphoreType.DMA,
            pltpu.SemaphoreType.DMA,
            pltpu.SemaphoreType.DMA,
            pltpu.SemaphoreType.DMA,
            pltpu.SemaphoreType.DMA,
        ],
        compiler_params=pltpu.CompilerParams(collective_id=0, has_side_effects=True),
    )(
        inverse_set.reshape(256, 128),
        presence.reshape(1, 2),
        factor.reshape(128, 512),
    )
    return (-update).reshape(1, 1, 8, 512), dinv + diag_sum


def solution(mesh):
    in_specs = (
        P(None, "row", None, None, "col", None),
        P(None, "row", None, "col"),
        P(None, "row", None, None),
        P("row", "col"),
    )
    out_specs = (P(None, "row", "col", None), P("row", "col"))
    return jax.shard_map(local, mesh=mesh, in_specs=in_specs, out_specs=out_specs, check_vma=False)
```

time: 1120 us -> 52.3 us (0.05)
  the two profiles are of different devices: /device:TPU:1 before, /device:TPU:4 now
where the time goes in v1:
time: 52.3 us; the launch traced here: 52.1 us
  Pallas kernels  49.5 us (95%)
  other arithmetic  1.94 us (4%)
  between operations  0.66 us (1%)
    pallas_call x1, Pallas kernels, local(): pl.pallas_call(kernel, out_shape=(jax.ShapeDtypeStruct((8, 512), F32), ja...  49.5 us
    reshape x1, other arithmetic, local(): return ((-update).reshape(1, 1, 8, 512), dinv + diag_sum)  1.34 us

profile of v1, /device:TPU:4, one launch (start us, length us, event | category | flops | bytes accessed | tf_op | source)
XLA Modules:
  0.0 52.1 jit_solution(17364507524298543268)
XLA Ops:
  0.6 49.5 %shard_map.59 = (f32[8,512]{1,0:T(8,128)}, f32[16,32]{1,0:T(8,128)}) custom-call(f32[256,128]{1,0:T(8,128)} %bitcast.6, s32[1,2]{1,0:T(1,128)} %bitcast.7, f32[128,512]{1,0:T(8,128)} %bitcast.5), custom_call_target="tpu_custom_call" | custom-call | tf_op jit(solution)/shard_map/pallas_call | solution.py:252
  50.1 0.0 copy-start
  50.1 0.0 copy-start.1
  50.2 1.3 %negate_bitcast_fusion = f32[1,1,8,512]{3,2,1,0:T(8,128)} fusion(f32[8,512]{1,0:T(8,128)} %get-tuple-element.4), kind=kLoop, calls=%fused_computation | loop fusion | flops 4096 | bytes 32768 | tf_op jit(solution)/shard_map/reshape | solution.py:290
  51.5 0.0 copy-done
  51.5 0.0 copy-done.1
  51.5 0.6 %add.3 = f32[16,32]{1,0:T(8,128)} add(f32[16,32]{1,0:T(8,128)S(1)} %copy-done, f32[16,32]{1,0:T(8,128)S(1)} %copy-done.1) | non-fusion elementwise | flops 512 | bytes 6144 | tf_op jit(solution)/shard_map/add | solution.py:290
Async XLA Ops:
  50.1 1.4 %copy-start = (f32[16,32]{1,0:T(8,128)S(1)}, f32[16,32]{1,0:T(8,128)}, u32[]{:S(2)}) copy-start(f32[16,32]{1,0:T(8,128)} %param.7) | copy-start | bytes 6148
  50.1 1.4 %copy-start.1 = (f32[16,32]{1,0:T(8,128)S(1)}, f32[16,32]{1,0:T(8,128)}, u32[]{:S(2)}) copy-start(f32[16,32]{1,0:T(8,128)} %get-tuple-element.5) | copy-start | bytes 6148

commit v2 on v0

v2 whole, which is shorter than its diff:
```python
import jax
import jax.numpy as jnp
from jax import lax
from jax.experimental import pallas as pl
from jax.experimental.pallas import tpu as pltpu
from jax.sharding import PartitionSpec as P

MESH = pl.DeviceIdType.MESH
NROW = 32
NCOL = 16
F32 = jnp.float32
BF16 = jnp.bfloat16
NT = (((1,), (1,)), ((), ()))
JUMP = 5
PLANE = [(dx, dy) for dx in range(2) for dy in range(4)]


def split(value):
    high = value.astype(BF16)
    return high, (value - high.astype(F32)).astype(BF16)


def dot_nt(a, b):
    return lax.dot_general(a, b, NT, preferred_element_type=F32)


def kernel(
    inv_hbm, pres_ref, fac_hbm, off_ref, diag_ref,
    a_raw, f_raw, ft, abuf, fbuf, fsplit, ftsplit, pad, q, trecv, vbuf, vrecv, mate, drecv,
    load_sem, f_send, f_first, f_rest, a_send, a_even, a_odd, t_send, t_recv, v_send, v_recv, d_send, d_recv,
):
    r = lax.axis_index("row")
    c = lax.axis_index("col")
    xh = lax.rem(r, 2)
    core = lax.rem(c, 2)
    y = lax.rem(lax.div(c, 2), 4)
    xl = lax.div(c, 8)
    chip = lax.div(c, 2)
    r_pair = r + 1 - 2 * xh
    c_cross = lax.rem(c + 8, NCOL)

    load_a = pltpu.make_async_copy(inv_hbm, a_raw, load_sem.at[0])
    load_f = pltpu.make_async_copy(fac_hbm, f_raw, load_sem.at[1])

    def send(src, dst, send_sem, recv_sem, peer):
        pltpu.make_async_remote_copy(
            src_ref=src, dst_ref=dst, send_sem=send_sem, recv_sem=recv_sem,
            device_id=peer, device_id_type=MESH,
        ).start()

    def wait(ref, sem):
        pltpu.make_async_copy(ref, ref, sem).wait()

    def at_plane(dx, dy, of_core):
        return lax.rem(xl + dx, 2) * 8 + lax.rem(y + dy, 4) * 2 + of_core

    def row_off(base, dz):
        return lax.rem(base + 2 * dz + NROW, NROW)

    def mask_own():
        load_a.wait()
        for b in range(2):
            abuf[c, b] = a_raw[pl.ds(b, 128, stride=2), :] * pres_ref[0, b].astype(F32)

    barrier = pltpu.get_barrier_semaphore()

    def greet(peer):
        pl.semaphore_signal(barrier, inc=1, device_id=peer, device_id_type=MESH)

    def put_update():
        for h in range(4):
            off_ref[:, 128 * h : 128 * (h + 1)] = vrecv[2 * h] + vrecv[2 * h + 1]

    @pl.when(core == 1)
    def _():
        load_a.start()
        mask_own()
        pl.semaphore_wait(barrier, 8)
        for dx, dy in reversed(PLANE):
            there = dx * 4 + (4 - dy) % 4
            send(abuf.at[c], abuf.at[c], a_send, a_odd.at[there], (r, at_plane(dx, dy, 0)))
        wait(vrecv, v_recv)
        put_update()
        wait(drecv, d_recv)
        diag_ref[...] = drecv[...]
        wait(abuf.at[pl.ds(0, 8)], a_send)

    @pl.when(core == 0)
    def _():
        load_f.start()
        load_a.start()
        for dx, dy in PLANE:
            greet((r, at_plane(dx, dy, 1)))
            if (dx, dy) != (0, 0):
                greet((r, at_plane(dx, dy, 0)))
        for dz in (5, 3, 2, 1):
            greet((row_off(r, dz), c))
            greet((row_off(r, -dz), c))
        for dz in (5, 2, 1):
            greet((row_off(r_pair, dz), c_cross))
            greet((row_off(r_pair, -dz), c_cross))
        greet((r_pair, c_cross))

        load_f.wait()
        for part in range(4):
            ft[128 * part : 128 * (part + 1), :] = f_raw[:, 128 * part : 128 * (part + 1)].T
        own_rows = pl.ds(pl.multiple_of(32 * c, 64), 64)
        cross_rows = pl.ds(pl.multiple_of(32 * c_cross, 64), 64)
        fbuf[r] = ft[own_rows, :]
        mask_own()
        pl.semaphore_wait(barrier, 22)

        def seed(dz, first):
            if dz:
                send(ft.at[own_rows, :], fbuf.at[r], f_send, first[0], (row_off(r, dz), c))
            send(ft.at[cross_rows, :], fbuf.at[r], f_send, first[1], (row_off(r_pair, dz), c_cross))

        seed(JUMP, (f_first.at[0, 0], f_first.at[0, 1]))
        seed(-JUMP, (f_first.at[1, 0], f_first.at[1, 1]))
        for dx, dy in reversed(PLANE[1:]):
            send(abuf.at[c], abuf.at[c], a_send, a_even, (r, at_plane(dx, dy, 0)))
        for dz in (2, -2, 1, -1, 0):
            seed(dz, (f_rest, f_rest))

        for g in range(2):
            high, low = split(ft[pl.ds(g, 256, stride=2), :])
            ftsplit[0:256, 128 * g : 128 * (g + 1)] = high
            ftsplit[256:512, 128 * g : 128 * (g + 1)] = low
        pad[...] = jnp.zeros_like(pad)

        bases = (r, r_pair)
        for chunk in range(2):
            for way in range(2):
                sign = 1 - 2 * way
                at = row_off(bases[chunk], -sign * JUMP)
                wait(fbuf.at[at], f_first.at[way, chunk])
                steps = [3 * sign] if way == chunk else []
                for dz in steps + [2 * sign, -2 * sign, sign, -sign]:
                    send(fbuf.at[at], fbuf.at[at], f_send, f_rest, (row_off(r, dz), c))

        wait(abuf.at[pl.ds(0, 7)], a_even)
        wait(fbuf.at[pl.ds(0, 27)], f_rest)

        def lay(at, carry):
            high, low = split(fbuf[at])
            place = (lax.rem(at, 2) * 8 + lax.div(lax.rem(at, NCOL), 2)) * 2 + lax.div(at, NCOL)
            lanes = pl.ds(pl.multiple_of(128 * place, 128), 128)
            fsplit[0:64, lanes] = high
            fsplit[64:128, lanes] = low
            return carry

        lax.fori_loop(0, NROW, lay, 0)

        def product(total, dx, dy, of_core):
            col = at_plane(dx, dy, of_core)
            both = jnp.concatenate([abuf[col, 0], abuf[col, 1]], axis=1)
            rhs = jnp.concatenate(split(both), axis=0)
            lanes = pl.ds(pl.multiple_of((of_core * 8 + lax.div(col, 2)) * 256, 256), 256)
            return total + dot_nt(fsplit[:, lanes], rhs)

        total = jnp.zeros((128, 256), F32)
        for dx, dy in PLANE:
            total = product(total, dx, dy, 0)
        for dx, dy in ((0, 0), (1, 0), (0, 1), (0, 3), (1, 1), (1, 3), (0, 2), (1, 2)):
            wait(abuf.at[0], a_odd.at[dx * 4 + dy])
            total = product(total, dx, dy, 1)
        part = total[:64, :128] + (total[:64, 128:] + total[64:, :128])

        high, low = split(part)
        zero = jnp.zeros((64, 128), BF16)
        rhs = jnp.concatenate(
            [
                jnp.concatenate([high, zero, low, zero], axis=0),
                jnp.concatenate([zero, high, zero, low], axis=0),
            ],
            axis=1,
        )
        full = dot_nt(ftsplit[...], rhs)
        q[...] = (full[:256, :128] + (full[:256, 128:] + full[256:, :128])).reshape(NROW, 8, 128)
        far_first = sorted(range(1, NROW), key=lambda step: -min(step // 2, 16 - step // 2))
        for step in far_first:
            goal = lax.rem(r + step, NROW)
            send(q.at[goal], trecv.at[step - 1], t_send, t_recv, (goal, c))

        pad[pl.ds(pl.multiple_of(64 * lax.rem(chip, 2), 64), 64), :] = part
        vbuf[...] = pad[...].T
        vrecv[chip] = vbuf[pl.ds(pl.multiple_of(8 * c, 8), 8), :]
        for dx, dy in reversed(PLANE):
            for of_core in range(2):
                if (dx, dy, of_core) != (0, 0, 0):
                    col = at_plane(dx, dy, of_core)
                    rows = pl.ds(pl.multiple_of(8 * col, 8), 8)
                    send(vbuf.at[rows, :], vrecv.at[chip], v_send, v_recv, (r, col))

        wait(vrecv.at[pl.ds(0, 7)], v_recv)
        put_update()

        wait(trecv, t_recv)
        tile = q[r]
        for step in range(NROW - 1):
            tile = tile + trecv[step]
        for g in range(2):
            mate[pl.ds(g, 8, stride=2), :] = tile[:, 64 * g + 32 : 64 * g + 64]
            diag_ref[pl.ds(g, 8, stride=2), :] = tile[:, 64 * g : 64 * g + 32]
        send(mate, drecv, d_send, d_recv, (r, c + 1))

        wait(fbuf.at[pl.ds(0, 31)], f_send)
        wait(abuf.at[pl.ds(0, 7)], a_send)
        wait(q.at[pl.ds(0, 31)], t_send)
        wait(vbuf.at[pl.ds(0, 120), :], v_send)
        wait(mate, d_send)


def local(inverse_set, presence, factor, dinv):
    update, diag_sum = pl.pallas_call(
        kernel,
        out_shape=(jax.ShapeDtypeStruct((8, 512), F32), jax.ShapeDtypeStruct((16, 32), F32)),
        in_specs=[
            pl.BlockSpec(memory_space=pl.ANY),
            pl.BlockSpec(memory_space=pltpu.SMEM),
            pl.BlockSpec(memory_space=pl.ANY),
        ],
        out_specs=(pl.BlockSpec(memory_space=pltpu.VMEM), pl.BlockSpec(memory_space=pltpu.VMEM)),
        scratch_shapes=[
            pltpu.VMEM((256, 128), F32),
            pltpu.VMEM((128, 512), F32),
            pltpu.VMEM((512, 128), F32),
            pltpu.VMEM((NCOL, 2, 128, 128), F32),
            pltpu.VMEM((NROW, 64, 128), F32),
            pltpu.VMEM((128, 4096), BF16),
            pltpu.VMEM((512, 256), BF16),
            pltpu.VMEM((128, 128), F32),
            pltpu.VMEM((NROW, 8, 128), F32),
            pltpu.VMEM((NROW - 1, 8, 128), F32),
            pltpu.VMEM((128, 128), F32),
            pltpu.VMEM((8, 8, 128), F32),
            pltpu.VMEM((16, 32), F32),
            pltpu.VMEM((16, 32), F32),
            pltpu.SemaphoreType.DMA((2,)),
            pltpu.SemaphoreType.DMA,
            pltpu.SemaphoreType.DMA((2, 2)),
            pltpu.SemaphoreType.DMA,
            pltpu.SemaphoreType.DMA,
            pltpu.SemaphoreType.DMA,
            pltpu.SemaphoreType.DMA((8,)),
            pltpu.SemaphoreType.DMA,
            pltpu.SemaphoreType.DMA,
            pltpu.SemaphoreType.DMA,
            pltpu.SemaphoreType.DMA,
            pltpu.SemaphoreType.DMA,
            pltpu.SemaphoreType.DMA,
        ],
        compiler_params=pltpu.CompilerParams(collective_id=0, has_side_effects=True),
    )(
        inverse_set.reshape(256, 128),
        presence.reshape(1, 2),
        factor.reshape(128, 512),
    )
    return (-update).reshape(1, 1, 8, 512), dinv + diag_sum


def solution(mesh):
    in_specs = (
        P(None, "row", None, None, "col", None),
        P(None, "row", None, "col"),
        P(None, "row", None, None),
        P("row", "col"),
    )
    out_specs = (P(None, "row", "col", None), P("row", "col"))
    return jax.shard_map(local, mesh=mesh, in_specs=in_specs, out_specs=out_specs, check_vma=False)
```

time: 1120 us -> 46.8 us (0.04); the launches traced: 1110 us -> 46.6 us
  waiting for transfers between devices: 1080 us -> 0 us
  Pallas kernels: 0 us -> 44 us
  between operations: 13.8 us -> 0.66 us
    unnamed x5 -> x0, waiting for transfers between devices: 633 us -> none
    psum x1 -> x0, waiting for transfers between devices: 295 us -> none  [spread(): return lax.psum(jnp.where(mine, value, jnp.zeros_like(value)), axis)]
    reduce_scatter x2 -> x0, waiting for transfers between devices: 152 us -> none  [the longest x1 84.6 us: local(): lax.psum_scatter(partial_value, 'col', scatter_dimension=1, tiled=True)]
    pallas_call x0 -> x1, Pallas kernels: none -> 44 us  [local(): pl.pallas_call(kernel, out_shape=(jax.ShapeDtypeStruct((8, 512), F32), ja...]
  transfers between devices with their start and end apart: 4 -> 0, of which waited for: 4 -> 0; matrix products, arithmetic and copies ran while one was open for 0% -> 0% of each run, Pallas kernels for 0% -> 0%
where the time goes in v2:
time: 46.8 us; the launch traced here: 46.6 us
  Pallas kernels  44 us (94%)
  other arithmetic  1.94 us (4%)
  between operations  0.66 us (1%)
    pallas_call x1, Pallas kernels, local(): pl.pallas_call(kernel, out_shape=(jax.ShapeDtypeStruct((8, 512), F32), ja...  44 us
    reshape x1, other arithmetic, local(): return ((-update).reshape(1, 1, 8, 512), dinv + diag_sum)  1.34 us

profile of v2, /device:TPU:1, one launch (start us, length us, event | category | flops | bytes accessed | tf_op | source)
XLA Modules:
  0.0 46.6 jit_solution(5012294802788134189)
XLA Ops:
  0.6 44.0 %shard_map.59 = (f32[8,512]{1,0:T(8,128)}, f32[16,32]{1,0:T(8,128)}) custom-call(f32[256,128]{1,0:T(8,128)} %bitcast.6, s32[1,2]{1,0:T(1,128)} %bitcast.7, f32[128,512]{1,0:T(8,128)} %bitcast.5), custom_call_target="tpu_custom_call" | custom-call | tf_op jit(solution)/shard_map/pallas_call | solution.py:215
  44.6 0.0 copy-start
  44.6 0.0 copy-start.1
  44.6 1.3 %negate_bitcast_fusion = f32[1,1,8,512]{3,2,1,0:T(8,128)} fusion(f32[8,512]{1,0:T(8,128)} %get-tuple-element.4), kind=kLoop, calls=%fused_computation | loop fusion | flops 4096 | bytes 32768 | tf_op jit(solution)/shard_map/reshape | solution.py:259
  45.9 0.0 copy-done
  46.0 0.0 copy-done.1
  46.0 0.6 %add.3 = f32[16,32]{1,0:T(8,128)} add(f32[16,32]{1,0:T(8,128)S(1)} %copy-done, f32[16,32]{1,0:T(8,128)S(1)} %copy-done.1) | non-fusion elementwise | flops 512 | bytes 6144 | tf_op jit(solution)/shard_map/add | solution.py:259
Async XLA Ops:
  44.6 1.4 %copy-start = (f32[16,32]{1,0:T(8,128)S(1)}, f32[16,32]{1,0:T(8,128)}, u32[]{:S(2)}) copy-start(f32[16,32]{1,0:T(8,128)} %param.7) | copy-start | bytes 6148
  44.6 1.4 %copy-start.1 = (f32[16,32]{1,0:T(8,128)S(1)}, f32[16,32]{1,0:T(8,128)}, u32[]{:S(2)}) copy-start(f32[16,32]{1,0:T(8,128)} %get-tuple-element.5) | copy-start | bytes 6148

commit v3 on v0

v3 whole, which is shorter than its diff:
```python
import jax
import jax.numpy as jnp
from jax import lax
from jax.experimental import pallas as pl
from jax.experimental.pallas import tpu as pltpu
from jax.sharding import PartitionSpec as P

MESH = pl.DeviceIdType.MESH
NROW = 32
F32 = jnp.float32
BF16 = jnp.bfloat16
NT = (((1,), (1,)), ((), ()))
JUMP = 5


def split(value):
    high = value.astype(BF16)
    return high, (value - high.astype(F32)).astype(BF16)


def dot_nt(a, b):
    return lax.dot_general(a, b, NT, preferred_element_type=F32)


def kernel(
    inv_hbm, pres_ref, fac_hbm, off_ref, diag_ref,
    a_raw, a_own, f_raw, ft, ft_mate, abuf, asplit, fbuf, ftsplit, pad, q, trecv, vbuf, vrecv,
    ready, load_sem, f_send, f_first, f_near, f_far, x_send, x_recv, a_send, a_recv,
    t_send, t_recv, v_send, v_recv,
):
    r = lax.axis_index("row")
    c = lax.axis_index("col")
    xh = lax.rem(r, 2)
    z = lax.div(r, 2)
    core = lax.rem(c, 2)
    y = lax.rem(lax.div(c, 2), 4)
    xl = lax.div(c, 8)
    chip = lax.div(c, 2)
    r_pair = r + 1 - 2 * xh

    load_a = pltpu.make_async_copy(inv_hbm, a_raw, load_sem.at[0])
    load_f = pltpu.make_async_copy(fac_hbm, f_raw, load_sem.at[1])

    def send(src, dst, send_sem, recv_sem, peer):
        pltpu.make_async_remote_copy(
            src_ref=src, dst_ref=dst, send_sem=send_sem, recv_sem=recv_sem,
            device_id=peer, device_id_type=MESH,
        ).start()

    def wait(ref, sem):
        pltpu.make_async_copy(ref, ref, sem).wait()

    halves = (xh, xh, 1 - xh, 1 - xh)
    lows = (xl, 1 - xl, 1 - xl, xl)
    rows = (r, r, r_pair, r_pair)

    def column_at(kind, dy, of_core):
        return lows[kind] * 8 + lax.rem(y + dy + 4, 4) * 2 + of_core

    def slot(kind, dy):
        return (halves[kind] * 2 + lows[kind]) * 4 + lax.rem(y + dy + 4, 4)

    def z_peer(dz):
        return (lax.rem(r + 2 * dz + NROW, NROW), c)

    def block_in():
        load_a.wait()
        for b in range(2):
            a_own[b] = a_raw[pl.ds(b, 128, stride=2), :] * pres_ref[0, b].astype(F32)

    def give(kind, dy, own):
        send(
            a_own, abuf.at[own], a_send, a_recv.at[kind, (4 - dy) % 4],
            (rows[kind], column_at(kind, dy, 0)),
        )

    def give_same_half(own):
        for dy in (1, -1):
            give(0, dy, own)
        for dy in (1, -1, 0):
            give(1, dy, own)

    def give_other_half(own):
        for dy in (1, -1, 0):
            give(2, dy, own)

    barrier = pltpu.get_barrier_semaphore()

    def greet(peer):
        pl.semaphore_signal(barrier, inc=1, device_id=peer, device_id_type=MESH)

    def put_update():
        for h in range(4):
            off_ref[:, 128 * h : 128 * (h + 1)] = (
                vrecv[2 * h] + vrecv[2 * h + 1] + (vrecv[2 * h + 8] + vrecv[2 * h + 9])
            )

    def put_diag():
        tile = trecv[0]
        for step in range(1, NROW):
            tile = tile + trecv[step]
        for g in range(4):
            diag_ref[pl.ds(g, 4, stride=4), :] = tile[:, 32 * g : 32 * (g + 1)]

    @pl.when(core == 1)
    def _():
        load_a.start()
        greet((r_pair, c))
        pl.semaphore_wait(barrier, 11)
        pl.semaphore_signal(ready, inc=1, device_id=(r, c - 1), device_id_type=MESH)
        block_in()
        own = slot(0, 0)

        @pl.when(xh == 1)
        def _():
            give_same_half(own)
            give(0, 0, own)

        @pl.when(xh == 0)
        def _():
            give_other_half(own)

        wait(vrecv, v_recv)
        put_update()
        wait(trecv, t_recv)
        put_diag()
        wait(abuf.at[pl.ds(0, 3)], a_send)

        @pl.when(xh == 1)
        def _():
            wait(abuf.at[pl.ds(0, 3)], a_send)

    @pl.when(core == 0)
    def _():
        load_a.start()
        load_f.start()
        for kind in range(3):
            for dy in (1, -1, 0):
                greet((rows[kind], column_at(kind, dy, 1)))
        greet((r_pair, c + 1))
        for dz in range(1, JUMP + 1):
            greet(z_peer(dz))
            greet(z_peer(-dz))

        block_in()
        own = slot(0, 0)
        pl.semaphore_wait(ready, 1)

        @pl.when(xh == 0)
        def _():
            give_same_half(own)
            abuf[own] = a_own[...]

        @pl.when(xh == 1)
        def _():
            give_other_half(own)

        load_f.wait()
        for part in range(4):
            ft[128 * part : 128 * (part + 1), :] = f_raw[:, 128 * part : 128 * (part + 1)].T
        own_rows = pl.ds(pl.multiple_of(32 * c, 64), 64)
        fbuf[z] = ft[own_rows, :]
        pl.semaphore_wait(barrier, 2 * JUMP)

        for way, dz in enumerate((JUMP, -JUMP)):
            send(ft.at[own_rows, :], fbuf.at[z], f_send, f_first.at[way], z_peer(dz))
        for dz in (4, -4, 3, -3, 2, -2, 1, -1):
            send(ft.at[own_rows, :], fbuf.at[z], f_send, f_near, z_peer(dz))
        send(ft, ft_mate, x_send, x_recv, (r_pair, column_at(2, 0, 0)))

        def lay_factor(source, at):
            for g in range(4):
                high, low = split(source[pl.ds(g, 128, stride=4), :])
                ftsplit[0:128, 128 * (4 * at + g) : 128 * (4 * at + g + 1)] = high
                ftsplit[128:256, 128 * (4 * at + g) : 128 * (4 * at + g + 1)] = low

        lay_factor(ft, 0)
        pad[...] = jnp.zeros_like(pad)

        def got(kind, dy):
            wait(abuf.at[slot(kind, dy)], a_recv.at[kind, dy % 4])

        def pass_half(kind, dy):
            b = 0 if dy == -1 else 1
            at = slot(kind, dy)
            send(
                abuf.at[at, b], abuf.at[at, b], a_send, a_recv.at[kind, 2 if b == 0 else 4],
                (r, column_at(0, -dy, 0)),
            )

        def pass_across(dy):
            at = slot(2, dy)
            send(abuf.at[at], abuf.at[at], a_send, a_recv.at[3, dy % 4], (r, column_at(1, 0, 0)))

        for dy in (-1, 1):
            got(2, dy)
            pass_across(dy)
            pass_half(2, dy)
        for dy in (-1, 1):
            got(0, dy)
            pass_half(0, dy)
        got(2, 0)
        pass_across(0)
        for dy in (-1, 1):
            got(1, dy)
            pass_half(1, dy)

        for way in range(2):
            sign = 1 - 2 * way
            at = lax.rem(z - sign * JUMP + 16, 16)
            wait(fbuf.at[at], f_first.at[way])
            half = fbuf.at[at, pl.ds(32 * way, 32)]
            send(half, half, f_send, f_far, z_peer(3 * sign))
            for dz in (2 * sign, sign):
                send(fbuf.at[at], fbuf.at[at], f_send, f_far, z_peer(dz))

        for dy in (-1, 1):
            got(3, dy)
            pass_half(3, dy)
        got(1, 0)
        got(3, 0)

        @pl.when(xh == 1)
        def _():
            got(0, 0)

        for kind in range(4):
            for b in range(2):
                wait(abuf.at[slot(kind, 2), b], a_recv.at[kind, 2 if b == 0 else 4])
        wait(ft_mate, x_recv)
        lay_factor(ft_mate, 1)

        def lay_blocks(p, carry):
            for at, half in enumerate((xh, 1 - xh)):
                for b in range(2):
                    high, low = split(abuf[half * 8 + p, b])
                    asplit[2 * p + b, 256 * at : 256 * at + 128] = high
                    asplit[2 * p + b, 256 * at + 128 : 256 * at + 256] = low
            return carry

        lax.fori_loop(0, 8, lay_blocks, 0)

        def product(dz):
            at = lax.rem(z + dz + 16, 16)
            lhs = jnp.concatenate(split(fbuf[at]), axis=0)
            return dot_nt(lhs, asplit[lax.rem(at, 8) * 2 + lax.div(at, 8)])

        wait(fbuf.at[pl.ds(0, 8)], f_near)
        total = product(0)
        for dz in range(1, 6):
            total = total + product(dz) + product(-dz)
        wait(fbuf.at[pl.ds(0, 5)], f_far)
        for dz in (6, -6, 7, -7, 8):
            total = total + product(dz)
        parts = [
            total[:64, 256 * at : 256 * at + 128]
            + (total[:64, 256 * at + 128 : 256 * at + 256] + total[64:, 256 * at : 256 * at + 128])
            for at in range(2)
        ]

        stacks = []
        for part in parts:
            pieces = split(part)
            for g in range(4):
                stack = []
                for of_core in range(2):
                    for piece in pieces:
                        for lane in range(4):
                            here = piece[32 * of_core : 32 * of_core + 32]
                            stack.append(here if lane == g else jnp.zeros((32, 128), BF16))
                stacks.append(jnp.concatenate(stack, axis=0))
        full = dot_nt(ftsplit[...], jnp.concatenate(stacks, axis=1))
        for of_core in range(2):
            left = 256 * of_core
            tiles = full[:128, left : left + 128] + (full[:128, left + 128 : left + 256] + full[128:, left : left + 128])
            q[:, of_core] = tiles.reshape(NROW, 4, 128)
        for at in range(NROW - 1):
            goal = at + (r <= at).astype(jnp.int32)
            step = lax.rem(goal - r + NROW, NROW)
            for of_core in range(2):
                send(q.at[goal, of_core], trecv.at[step], t_send, t_recv, (goal, c + of_core))
        send(q.at[r, 1], trecv.at[0], t_send, t_recv, (r, c + 1))
        trecv[0] = q[r, 0]

        half_rows = pl.ds(pl.multiple_of(64 * lax.rem(chip, 2), 64), 64)
        mine = xh * 8 + chip
        for which in range(2):
            pad[which, half_rows, :] = parts[which]
            vbuf[which] = pad[which].T
        vrecv[mine] = vbuf[0, pl.ds(pl.multiple_of(8 * c, 8), 8), :]
        for kind in (3, 2, 1, 0):
            for dy in (2, 3, 1, 0):
                for of_core in range(2):
                    if (kind, dy, of_core) != (0, 0, 0):
                        col = column_at(kind, dy, of_core)
                        slab = vbuf.at[kind // 2, pl.ds(pl.multiple_of(8 * col, 8), 8), :]
                        send(slab, vrecv.at[mine], v_send, v_recv, (rows[kind], col))

        wait(vrecv.at[pl.ds(0, 15)], v_recv)
        put_update()

        wait(trecv.at[pl.ds(1, 31)], t_recv)
        put_diag()

        wait(fbuf.at[pl.ds(0, 15)], f_send)
        wait(ft, x_send)
        wait(abuf.at[pl.ds(0, 10)], a_send)

        @pl.when(xh == 0)
        def _():
            wait(abuf.at[pl.ds(0, 2)], a_send)

        wait(q.at[pl.ds(0, 31)], t_send)
        wait(trecv.at[0], t_send)
        wait(vrecv.at[pl.ds(0, 16)], v_send)
        wait(vrecv.at[pl.ds(0, 15)], v_send)


def local(inverse_set, presence, factor, dinv):
    update, diag_sum = pl.pallas_call(
        kernel,
        out_shape=(jax.ShapeDtypeStruct((8, 512), F32), jax.ShapeDtypeStruct((16, 32), F32)),
        in_specs=[
            pl.BlockSpec(memory_space=pl.ANY),
            pl.BlockSpec(memory_space=pltpu.SMEM),
            pl.BlockSpec(memory_space=pl.ANY),
        ],
        out_specs=(pl.BlockSpec(memory_space=pltpu.VMEM), pl.BlockSpec(memory_space=pltpu.VMEM)),
        scratch_shapes=[
            pltpu.VMEM((256, 128), F32),
            pltpu.VMEM((2, 128, 128), F32),
            pltpu.VMEM((128, 512), F32),
            pltpu.VMEM((512, 128), F32),
            pltpu.VMEM((512, 128), F32),
            pltpu.VMEM((16, 2, 128, 128), F32),
            pltpu.VMEM((16, 512, 128), BF16),
            pltpu.VMEM((16, 64, 128), F32),
            pltpu.VMEM((256, 1024), BF16),
            pltpu.VMEM((2, 128, 128), F32),
            pltpu.VMEM((NROW, 2, 4, 128), F32),
            pltpu.VMEM((NROW, 4, 128), F32),
            pltpu.VMEM((2, 128, 128), F32),
            pltpu.VMEM((16, 8, 128), F32),
            pltpu.SemaphoreType.REGULAR,
            pltpu.SemaphoreType.DMA((2,)),
            pltpu.SemaphoreType.DMA,
            pltpu.SemaphoreType.DMA((2,)),
            pltpu.SemaphoreType.DMA,
            pltpu.SemaphoreType.DMA,
            pltpu.SemaphoreType.DMA,
            pltpu.SemaphoreType.DMA,
            pltpu.SemaphoreType.DMA,
            pltpu.SemaphoreType.DMA((4, 5)),
            pltpu.SemaphoreType.DMA,
            pltpu.SemaphoreType.DMA,
            pltpu.SemaphoreType.DMA,
            pltpu.SemaphoreType.DMA,
        ],
        compiler_params=pltpu.CompilerParams(collective_id=0, has_side_effects=True),
    )(
        inverse_set.reshape(256, 128),
        presence.reshape(1, 2),
        factor.reshape(128, 512),
    )
    return (-update).reshape(1, 1, 8, 512), dinv + diag_sum


def solution(mesh):
    in_specs = (
        P(None, "row", None, None, "col", None),
        P(None, "row", None, "col"),
        P(None, "row", None, None),
        P("row", "col"),
    )
    out_specs = (P(None, "row", "col", None), P("row", "col"))
    return jax.shard_map(local, mesh=mesh, in_specs=in_specs, out_specs=out_specs, check_vma=False)
```

time: 1120 us -> 44.7 us (0.04); the launches traced: 1110 us -> 44.5 us
  waiting for transfers between devices: 1080 us -> 0 us
  Pallas kernels: 0 us -> 41.9 us
  between operations: 13.8 us -> 0.66 us
    unnamed x5 -> x0, waiting for transfers between devices: 633 us -> none
    psum x1 -> x0, waiting for transfers between devices: 295 us -> none  [spread(): return lax.psum(jnp.where(mine, value, jnp.zeros_like(value)), axis)]
    reduce_scatter x2 -> x0, waiting for transfers between devices: 152 us -> none  [the longest x1 84.6 us: local(): lax.psum_scatter(partial_value, 'col', scatter_dimension=1, tiled=True)]
    pallas_call x0 -> x1, Pallas kernels: none -> 41.9 us  [local(): pl.pallas_call(kernel, out_shape=(jax.ShapeDtypeStruct((8, 512), F32), ja...]
  transfers between devices with their start and end apart: 4 -> 0, of which waited for: 4 -> 0; matrix products, arithmetic and copies ran while one was open for 0% -> 0% of each run, Pallas kernels for 0% -> 0%
where the time goes in v3:
time: 44.7 us; the launch traced here: 44.5 us
  Pallas kernels  41.9 us (94%)
  other arithmetic  1.94 us (4%)
  between operations  0.66 us (1%)
    pallas_call x1, Pallas kernels, local(): pl.pallas_call(kernel, out_shape=(jax.ShapeDtypeStruct((8, 512), F32), ja...  41.9 us
    reshape x1, other arithmetic, local(): return ((-update).reshape(1, 1, 8, 512), dinv + diag_sum)  1.34 us

profile of v3, /device:TPU:1, one launch (start us, length us, event | category | flops | bytes accessed | tf_op | source)
XLA Modules:
  0.0 44.5 jit_solution(2985892349817081778)
XLA Ops:
  0.6 41.9 %shard_map.59 = (f32[8,512]{1,0:T(8,128)}, f32[16,32]{1,0:T(8,128)}) custom-call(f32[256,128]{1,0:T(8,128)} %bitcast.6, s32[1,2]{1,0:T(1,128)} %bitcast.7, f32[128,512]{1,0:T(8,128)} %bitcast.5), custom_call_target="tpu_custom_call" | custom-call | tf_op jit(solution)/shard_map/pallas_call | solution.py:320
  42.5 0.0 copy-start
  42.5 0.0 copy-start.1
  42.5 1.3 %negate_bitcast_fusion = f32[1,1,8,512]{3,2,1,0:T(8,128)} fusion(f32[8,512]{1,0:T(8,128)} %get-tuple-element.4), kind=kLoop, calls=%fused_computation | loop fusion | flops 4096 | bytes 32768 | tf_op jit(solution)/shard_map/reshape | solution.py:365
  43.9 0.0 copy-done
  43.9 0.0 copy-done.1
  43.9 0.6 %add.3 = f32[16,32]{1,0:T(8,128)} add(f32[16,32]{1,0:T(8,128)S(1)} %copy-done, f32[16,32]{1,0:T(8,128)S(1)} %copy-done.1) | non-fusion elementwise | flops 512 | bytes 6144 | tf_op jit(solution)/shard_map/add | solution.py:365
Async XLA Ops:
  42.5 1.4 %copy-start = (f32[16,32]{1,0:T(8,128)S(1)}, f32[16,32]{1,0:T(8,128)}, u32[]{:S(2)}) copy-start(f32[16,32]{1,0:T(8,128)} %param.7) | copy-start | bytes 6148
  42.5 1.4 %copy-start.1 = (f32[16,32]{1,0:T(8,128)S(1)}, f32[16,32]{1,0:T(8,128)}, u32[]{:S(2)}) copy-start(f32[16,32]{1,0:T(8,128)} %get-tuple-element.5) | copy-start | bytes 6148

commit v4 on v3

--- a/solution.py
+++ b/solution.py
@@ -68,21 +68,23 @@
         for b in range(2):
             a_own[b] = a_raw[pl.ds(b, 128, stride=2), :] * pres_ref[0, b].astype(F32)
 
-    def give(kind, dy, own):
+    def give(kind, dy, b, own):
         send(
-            a_own, abuf.at[own], a_send, a_recv.at[kind, (4 - dy) % 4],
+            a_own.at[b], abuf.at[own, b], a_send, a_recv.at[kind, (4 - dy) % 4, b],
             (rows[kind], column_at(kind, dy, 0)),
         )
 
     def give_same_half(own):
-        for dy in (1, -1):
-            give(0, dy, own)
-        for dy in (1, -1, 0):
-            give(1, dy, own)
+        for b in range(2):
+            for kind, dy in ((1, 0), (0, 1), (0, -1)):
+                give(kind, dy, b, own)
 
     def give_other_half(own):
-        for dy in (1, -1, 0):
-            give(2, dy, own)
+        for b in range(2):
+            for dy in (1, -1):
+                give(2, dy, b, own)
+        for b in range(2):
+            give(2, 0, b, own)
 
     barrier = pltpu.get_barrier_semaphore()
 
@@ -114,7 +116,8 @@
         @pl.when(xh == 1)
         def _():
             give_same_half(own)
-            give(0, 0, own)
+            for b in range(2):
+                give(0, 0, b, own)
 
         @pl.when(xh == 0)
         def _():
@@ -128,7 +131,7 @@
 
         @pl.when(xh == 1)
         def _():
-            wait(abuf.at[pl.ds(0, 3)], a_send)
+            wait(abuf.at[0], a_send)
 
     @pl.when(core == 0)
     def _():
@@ -177,33 +180,37 @@
         lay_factor(ft, 0)
         pad[...] = jnp.zeros_like(pad)
 
-        def got(kind, dy):
-            wait(abuf.at[slot(kind, dy)], a_recv.at[kind, dy % 4])
-
-        def pass_half(kind, dy):
-            b = 0 if dy == -1 else 1
+        def got(kind, dy, b):
+            wait(abuf.at[slot(kind, dy), b], a_recv.at[kind, dy % 4, b])
+
+        def pass_y(kind, dy, b, to):
             at = slot(kind, dy)
             send(
-                abuf.at[at, b], abuf.at[at, b], a_send, a_recv.at[kind, 2 if b == 0 else 4],
-                (r, column_at(0, -dy, 0)),
+                abuf.at[at, b], abuf.at[at, b], a_send, a_recv.at[kind, (dy - to) % 4, b],
+                (r, column_at(0, to, 0)),
             )
 
-        def pass_across(dy):
+        def pass_across(dy, b):
             at = slot(2, dy)
-            send(abuf.at[at], abuf.at[at], a_send, a_recv.at[3, dy % 4], (r, column_at(1, 0, 0)))
-
-        for dy in (-1, 1):
-            got(2, dy)
-            pass_across(dy)
-            pass_half(2, dy)
-        for dy in (-1, 1):
-            got(0, dy)
-            pass_half(0, dy)
-        got(2, 0)
-        pass_across(0)
-        for dy in (-1, 1):
-            got(1, dy)
-            pass_half(1, dy)
+            send(abuf.at[at, b], abuf.at[at, b], a_send, a_recv.at[3, dy % 4, b], (r, column_at(1, 0, 0)))
+
+        for b in range(2):
+            got(1, 0, b)
+            pass_y(1, 0, b, 1)
+            pass_y(1, 0, b, -1)
+            for dy in (-1, 1):
+                got(2, dy, b)
+                pass_across(dy, b)
+                if dy == 2 * b - 1:
+                    pass_y(2, dy, b, -dy)
+            got(0, 2 * b - 1, b)
+            pass_y(0, 2 * b - 1, b, 1 - 2 * b)
+        for b in range(2):
+            got(2, 0, b)
+            pass_across(0, b)
+        for b in range(2):
+            got(1, 2 * b - 1, b)
+            pass_y(1, 2 * b - 1, b, 1 - 2 * b)
 
         for way in range(2):
             sign = 1 - 2 * way
@@ -214,19 +221,21 @@
             for dz in (2 * sign, sign):
                 send(fbuf.at[at], fbuf.at[at], f_send, f_far, z_peer(dz))
 
-        for dy in (-1, 1):
-            got(3, dy)
-            pass_half(3, dy)
-        got(1, 0)
-        got(3, 0)
+        for b in range(2):
+            got(3, 2 * b - 1, b)
+            pass_y(3, 2 * b - 1, b, 1 - 2 * b)
 
         @pl.when(xh == 1)
         def _():
-            got(0, 0)
-
-        for kind in range(4):
             for b in range(2):
-                wait(abuf.at[slot(kind, 2), b], a_recv.at[kind, 2 if b == 0 else 4])
+                got(0, 0, b)
+
+        for b in range(2):
+            for kind in (0, 1, 3):
+                got(kind, 1 - 2 * b, b)
+            got(3, 0, b)
+            for kind in range(4):
+                got(kind, 2, b)
         wait(ft_mate, x_recv)
         lay_factor(ft_mate, 1)
 
@@ -304,12 +313,7 @@
 
         wait(fbuf.at[pl.ds(0, 15)], f_send)
         wait(ft, x_send)
-        wait(abuf.at[pl.ds(0, 10)], a_send)
-
-        @pl.when(xh == 0)
-        def _():
-            wait(abuf.at[pl.ds(0, 2)], a_send)
-
+        wait(abuf.at[pl.ds(0, 12)], a_send)
         wait(q.at[pl.ds(0, 31)], t_send)
         wait(trecv.at[0], t_send)
         wait(vrecv.at[pl.ds(0, 16)], v_send)
@@ -319,7 +323,7 @@
 def local(inverse_set, presence, factor, dinv):
     update, diag_sum = pl.pallas_call(
         kernel,
-        out_shape=(jax.ShapeDtypeStruct((8, 512), F32), jax.ShapeDtypeStruct((16, 32), F32)),
+        out_shape=(pltpu.VMEM((8, 512), F32), pltpu.VMEM((16, 32), F32)),
         in_specs=[
             pl.BlockSpec(memory_space=pl.ANY),
             pl.BlockSpec(memory_space=pltpu.SMEM),
@@ -350,7 +354,7 @@
             pltpu.SemaphoreType.DMA,
             pltpu.SemaphoreType.DMA,
             pltpu.SemaphoreType.DMA,
-            pltpu.SemaphoreType.DMA((4, 5)),
+            pltpu.SemaphoreType.DMA((4, 4, 2)),
             pltpu.SemaphoreType.DMA,
             pltpu.SemaphoreType.DMA,
             pltpu.SemaphoreType.DMA,

time: 44.7 us -> 42.5 us (0.951)
  Pallas kernels: 41.9 us -> 40.4 us
  other arithmetic: 1.94 us -> 1.21 us
    pallas_call x1, Pallas kernels: 41.9 us -> 40.4 us  [local(): pl.pallas_call(kernel, out_shape=(pltpu.VMEM((8, 512), F32), pltpu.VMEM((...]
    reshape x1, other arithmetic: 1.34 us -> 0.61 us  [local(): return ((-update).reshape(1, 1, 8, 512), dinv + diag_sum)]
where the time goes in v4:
time: 42.5 us; the launch traced here: 42.3 us
  Pallas kernels  40.4 us (95%)
  other arithmetic  1.21 us (3%)
  between operations  0.65 us (2%)
    pallas_call x1, Pallas kernels, local(): pl.pallas_call(kernel, out_shape=(pltpu.VMEM((8, 512), F32), pltpu.VMEM((...  40.4 us

profile of v4, /device:TPU:1, one launch (start us, length us, event | category | flops | bytes accessed | tf_op | source)
XLA Modules:
  0.0 42.3 jit_solution(5166089130561007720)
XLA Ops:
  0.6 40.4 %shard_map.59 = (f32[8,512]{1,0:T(8,128)S(1)}, f32[16,32]{1,0:T(8,128)S(1)}) custom-call(f32[256,128]{1,0:T(8,128)} %bitcast.6, s32[1,2]{1,0:T(1,128)} %bitcast.7, f32[128,512]{1,0:T(8,128)} %bitcast.5), custom_call_target="tpu_custom_call" | custom-call | tf_op jit(solution)/shard_map/pallas_call | solution.py:324
  41.0 0.0 copy-start
  41.0 0.6 %negate_bitcast_fusion = f32[1,1,8,512]{3,2,1,0:T(8,128)} fusion(f32[8,512]{1,0:T(8,128)S(1)} %get-tuple-element.4), kind=kLoop, calls=%fused_computation | loop fusion | flops 4096 | bytes 32768 | tf_op jit(solution)/shard_map/reshape | solution.py:369
  41.6 0.1 copy-done
  41.7 0.6 %add.3 = f32[16,32]{1,0:T(8,128)} add(f32[16,32]{1,0:T(8,128)S(1)} %copy-done, f32[16,32]{1,0:T(8,128)S(1)} %get-tuple-element.5) | non-fusion elementwise | flops 512 | bytes 6144 | tf_op jit(solution)/shard_map/add | solution.py:369
Async XLA Ops:
  41.0 0.7 %copy-start = (f32[16,32]{1,0:T(8,128)S(1)}, f32[16,32]{1,0:T(8,128)}, u32[]{:S(2)}) copy-start(f32[16,32]{1,0:T(8,128)} %param.7) | copy-start | bytes 6148

commit v5 on v4

--- a/solution.py
+++ b/solution.py
@@ -23,8 +23,8 @@
 
 
 def kernel(
-    inv_hbm, pres_ref, fac_hbm, off_ref, diag_ref,
-    a_raw, a_own, f_raw, ft, ft_mate, abuf, asplit, fbuf, ftsplit, pad, q, trecv, vbuf, vrecv,
+    inv_hbm, pres_ref, fac_hbm, dinv_hbm, off_ref, diag_ref,
+    a_raw, a_own, d_raw, f_raw, ft, ft_mate, abuf, asplit, fbuf, ftsplit, pad, q, trecv, vbuf, vrecv,
     ready, load_sem, f_send, f_first, f_near, f_far, x_send, x_recv, a_send, a_recv,
     t_send, t_recv, v_send, v_recv,
 ):
@@ -40,6 +40,7 @@
 
     load_a = pltpu.make_async_copy(inv_hbm, a_raw, load_sem.at[0])
     load_f = pltpu.make_async_copy(fac_hbm, f_raw, load_sem.at[1])
+    load_d = pltpu.make_async_copy(dinv_hbm, d_raw, load_sem.at[2])
 
     def send(src, dst, send_sem, recv_sem, peer):
         pltpu.make_async_remote_copy(
@@ -93,7 +94,7 @@
 
     def put_update():
         for h in range(4):
-            off_ref[:, 128 * h : 128 * (h + 1)] = (
+            off_ref[:, 128 * h : 128 * (h + 1)] = -(
                 vrecv[2 * h] + vrecv[2 * h + 1] + (vrecv[2 * h + 8] + vrecv[2 * h + 9])
             )
 
@@ -102,11 +103,13 @@
         for step in range(1, NROW):
             tile = tile + trecv[step]
         for g in range(4):
-            diag_ref[pl.ds(g, 4, stride=4), :] = tile[:, 32 * g : 32 * (g + 1)]
+            spots = pl.ds(g, 4, stride=4)
+            diag_ref[spots, :] = d_raw[spots, :] + tile[:, 32 * g : 32 * (g + 1)]
 
     @pl.when(core == 1)
     def _():
         load_a.start()
+        load_d.start()
         greet((r_pair, c))
         pl.semaphore_wait(barrier, 11)
         pl.semaphore_signal(ready, inc=1, device_id=(r, c - 1), device_id_type=MESH)
@@ -123,6 +126,7 @@
         def _():
             give_other_half(own)
 
+        load_d.wait()
         wait(vrecv, v_recv)
         put_update()
         wait(trecv, t_recv)
@@ -137,6 +141,7 @@
     def _():
         load_a.start()
         load_f.start()
+        load_d.start()
         for kind in range(3):
             for dy in (1, -1, 0):
                 greet((rows[kind], column_at(kind, dy, 1)))
@@ -169,7 +174,6 @@
             send(ft.at[own_rows, :], fbuf.at[z], f_send, f_first.at[way], z_peer(dz))
         for dz in (4, -4, 3, -3, 2, -2, 1, -1):
             send(ft.at[own_rows, :], fbuf.at[z], f_send, f_near, z_peer(dz))
-        send(ft, ft_mate, x_send, x_recv, (r_pair, column_at(2, 0, 0)))
 
         def lay_factor(source, at):
             for g in range(4):
@@ -178,6 +182,7 @@
                 ftsplit[128:256, 128 * (4 * at + g) : 128 * (4 * at + g + 1)] = low
 
         lay_factor(ft, 0)
+        load_d.wait()
         pad[...] = jnp.zeros_like(pad)
 
         def got(kind, dy, b):
@@ -221,6 +226,8 @@
             for dz in (2 * sign, sign):
                 send(fbuf.at[at], fbuf.at[at], f_send, f_far, z_peer(dz))
 
+        send(ft, ft_mate, x_send, x_recv, (r_pair, column_at(2, 0, 0)))
+
         for b in range(2):
             got(3, 2 * b - 1, b)
             pass_y(3, 2 * b - 1, b, 1 - 2 * b)
@@ -229,38 +236,43 @@
         def _():
             for b in range(2):
                 got(0, 0, b)
+
+        def lay_piece(kind, dy, b):
+            high, low = split(abuf[slot(kind, dy), b])
+            at = (lows[kind] * 4 + lax.rem(y + dy + 4, 4)) * 2 + b
+            left = 256 * (kind // 2)
+            asplit[at, left : left + 128] = high
+            asplit[at, left + 128 : left + 256] = low
+
+        def product(low_x, dy, b):
+            chip_at = low_x * 4 + lax.rem(y + dy + 4, 4)
+            lhs = jnp.concatenate(split(fbuf[chip_at + 8 * b]), axis=0)
+            return dot_nt(lhs, asplit[chip_at * 2 + b])
 
         for b in range(2):
             for kind in (0, 1, 3):
                 got(kind, 1 - 2 * b, b)
             got(3, 0, b)
-            for kind in range(4):
-                got(kind, 2, b)
+        for kind in range(4):
+            for dy in (0, 1, -1):
+                for b in range(2):
+                    lay_piece(kind, dy, b)
         wait(ft_mate, x_recv)
         lay_factor(ft_mate, 1)
-
-        def lay_blocks(p, carry):
-            for at, half in enumerate((xh, 1 - xh)):
+        wait(fbuf.at[pl.ds(0, 8)], f_near)
+        wait(fbuf.at[pl.ds(0, 5)], f_far)
+        total = jnp.zeros((128, 512), F32)
+        for low_x in (xl, 1 - xl):
+            for dy in (0, 1, -1):
                 for b in range(2):
-                    high, low = split(abuf[half * 8 + p, b])
-                    asplit[2 * p + b, 256 * at : 256 * at + 128] = high
-                    asplit[2 * p + b, 256 * at + 128 : 256 * at + 256] = low
-            return carry
-
-        lax.fori_loop(0, 8, lay_blocks, 0)
-
-        def product(dz):
-            at = lax.rem(z + dz + 16, 16)
-            lhs = jnp.concatenate(split(fbuf[at]), axis=0)
-            return dot_nt(lhs, asplit[lax.rem(at, 8) * 2 + lax.div(at, 8)])
-
-        wait(fbuf.at[pl.ds(0, 8)], f_near)
-        total = product(0)
-        for dz in range(1, 6):
-            total = total + product(dz) + product(-dz)
-        wait(fbuf.at[pl.ds(0, 5)], f_far)
-        for dz in (6, -6, 7, -7, 8):
-            total = total + product(dz)
+                    total = total + product(low_x, dy, b)
+        for kind in range(4):
+            for b in range(2):
+                got(kind, 2, b)
+                lay_piece(kind, 2, b)
+        for low_x in (xl, 1 - xl):
+            for b in range(2):
+                total = total + product(low_x, 2, b)
         parts = [
             total[:64, 256 * at : 256 * at + 128]
             + (total[:64, 256 * at + 128 : 256 * at + 256] + total[64:, 256 * at : 256 * at + 128])
@@ -321,18 +333,20 @@
 
 
 def local(inverse_set, presence, factor, dinv):
-    update, diag_sum = pl.pallas_call(
+    update, diag = pl.pallas_call(
         kernel,
         out_shape=(pltpu.VMEM((8, 512), F32), pltpu.VMEM((16, 32), F32)),
         in_specs=[
             pl.BlockSpec(memory_space=pl.ANY),
             pl.BlockSpec(memory_space=pltpu.SMEM),
             pl.BlockSpec(memory_space=pl.ANY),
+            pl.BlockSpec(memory_space=pl.ANY),
         ],
         out_specs=(pl.BlockSpec(memory_space=pltpu.VMEM), pl.BlockSpec(memory_space=pltpu.VMEM)),
         scratch_shapes=[
             pltpu.VMEM((256, 128), F32),
             pltpu.VMEM((2, 128, 128), F32),
+            pltpu.VMEM((16, 32), F32),
             pltpu.VMEM((128, 512), F32),
             pltpu.VMEM((512, 128), F32),
             pltpu.VMEM((512, 128), F32),
@@ -346,7 +360,7 @@
             pltpu.VMEM((2, 128, 128), F32),
             pltpu.VMEM((16, 8, 128), F32),
             pltpu.SemaphoreType.REGULAR,
-            pltpu.SemaphoreType.DMA((2,)),
+            pltpu.SemaphoreType.DMA((3,)),
             pltpu.SemaphoreType.DMA,
             pltpu.SemaphoreType.DMA((2,)),
             pltpu.SemaphoreType.DMA,
@@ -365,8 +379,9 @@
         inverse_set.reshape(256, 128),
         presence.reshape(1, 2),
         factor.reshape(128, 512),
+        dinv,
     )
-    return (-update).reshape(1, 1, 8, 512), dinv + diag_sum
+    return update.reshape(1, 1, 8, 512), diag
 
 
 def solution(mesh):

time: 42.5 us -> 40.5 us (0.953)
  Pallas kernels: 40.4 us -> 38.6 us
  other arithmetic: 1.21 us -> 0 us
  local copies, waits for them, and re-layouts: 0.08 us -> 1.21 us
    pallas_call x1, Pallas kernels: 40.4 us -> 38.6 us  [local(): pl.pallas_call(kernel, out_shape=(pltpu.VMEM((8, 512), F32), pltpu.VMEM((...]
    unnamed x2, local copies, waits for them, and re-layouts: 0.08 us -> 1.21 us
    reshape x1 -> x0, other arithmetic: 0.61 us -> none  [local(): return ((-update).reshape(1, 1, 8, 512), dinv + diag_sum)]
    add x1 -> x0, other arithmetic: 0.6 us -> none  [local(): return ((-update).reshape(1, 1, 8, 512), dinv + diag_sum)]
where the time goes in v5:
time: 40.5 us; the launch traced here: 40.4 us
  Pallas kernels  38.6 us (95%)
  local copies, waits for them, and re-layouts  1.21 us (3%)
  between operations  0.64 us (2%)
    pallas_call x1, Pallas kernels, local(): pl.pallas_call(kernel, out_shape=(pltpu.VMEM((8, 512), F32), pltpu.VMEM((...  38.6 us
    unnamed x2, local copies, waits for them, and re-layouts  1.21 us

profile of v5, /device:TPU:1, one launch (start us, length us, event | category | flops | bytes accessed | tf_op | source)
XLA Modules:
  0.0 40.4 jit_solution(15101220300431305)
XLA Ops:
  0.6 38.6 %shard_map.59 = (f32[8,512]{1,0:T(8,128)S(1)}, f32[16,32]{1,0:T(8,128)S(1)}) custom-call(f32[256,128]{1,0:T(8,128)} %bitcast.6, s32[1,2]{1,0:T(1,128)} %bitcast.7, f32[128,512]{1,0:T(8,128)} %bitcast.5, f32[16,32]{1,0:T(8,128)} %dinv_hbm.1), custom_call_target="tpu_custom_call" | custom-call | tf_op jit(solution)/shard_map/pallas_call | solution.py:336
  39.2 0.6 %copy.8 = f32[1,1,8,512]{3,2,1,0:T(8,128)} copy(f32[1,1,8,512]{3,2,1,0:T(8,128)S(1)} %bitcast.4) | data formatting | bytes 32768
  39.8 0.6 %copy.9 = f32[16,32]{1,0:T(8,128)} copy(f32[16,32]{1,0:T(8,128)S(1)} %get-tuple-element.7) | data formatting | bytes 4096

commit v6 on v5

--- a/solution.py
+++ b/solution.py
@@ -77,7 +77,7 @@
 
     def give_same_half(own):
         for b in range(2):
-            for kind, dy in ((1, 0), (0, 1), (0, -1)):
+            for kind, dy in ((1, 1 - 2 * b), (0, 1 - 2 * b), (1, 0), (0, 2 * b - 1)):
                 give(kind, dy, b, own)
 
     def give_other_half(own):
@@ -135,7 +135,7 @@
 
         @pl.when(xh == 1)
         def _():
-            wait(abuf.at[0], a_send)
+            wait(abuf.at[pl.ds(0, 2)], a_send)
 
     @pl.when(core == 0)
     def _():
@@ -201,8 +201,7 @@
 
         for b in range(2):
             got(1, 0, b)
-            pass_y(1, 0, b, 1)
-            pass_y(1, 0, b, -1)
+            pass_y(1, 0, b, 2 * b - 1)
             for dy in (-1, 1):
                 got(2, dy, b)
                 pass_across(dy, b)
@@ -298,7 +297,7 @@
         for at in range(NROW - 1):
             goal = at + (r <= at).astype(jnp.int32)
             step = lax.rem(goal - r + NROW, NROW)
-            for of_core in range(2):
+            for of_core in (1, 0):
                 send(q.at[goal, of_core], trecv.at[step], t_send, t_recv, (goal, c + of_core))
         send(q.at[r, 1], trecv.at[0], t_send, t_recv, (r, c + 1))
         trecv[0] = q[r, 0]
@@ -325,7 +324,12 @@
 
         wait(fbuf.at[pl.ds(0, 15)], f_send)
         wait(ft, x_send)
-        wait(abuf.at[pl.ds(0, 12)], a_send)
+        wait(abuf.at[pl.ds(0, 11)], a_send)
+
+        @pl.when(xh == 0)
+        def _():
+            wait(abuf.at[0], a_send)
+
         wait(q.at[pl.ds(0, 31)], t_send)
         wait(trecv.at[0], t_send)
         wait(vrecv.at[pl.ds(0, 16)], v_send)

time: 40.5 us -> 40.1 us (level)
  Pallas kernels: 38.6 us -> 38.1 us
    pallas_call x1, Pallas kernels: 38.6 us -> 38.1 us  [local(): pl.pallas_call(kernel, out_shape=(pltpu.VMEM((8, 512), F32), pltpu.VMEM((...]
where the time goes in v6:
time: 40.1 us; the launch traced here: 40 us
  Pallas kernels  38.1 us (95%)
  local copies, waits for them, and re-layouts  1.21 us (3%)
  between operations  0.64 us (2%)
    pallas_call x1, Pallas kernels, local(): pl.pallas_call(kernel, out_shape=(pltpu.VMEM((8, 512), F32), pltpu.VMEM((...  38.1 us
    unnamed x2, local copies, waits for them, and re-layouts  1.21 us

profile of v6, /device:TPU:1, one launch (start us, length us, event | category | flops | bytes accessed | tf_op | source)
XLA Modules:
  0.0 40.0 jit_solution(14612061567369406097)
XLA Ops:
  0.6 38.1 %shard_map.59 = (f32[8,512]{1,0:T(8,128)S(1)}, f32[16,32]{1,0:T(8,128)S(1)}) custom-call(f32[256,128]{1,0:T(8,128)} %bitcast.6, s32[1,2]{1,0:T(1,128)} %bitcast.7, f32[128,512]{1,0:T(8,128)} %bitcast.5, f32[16,32]{1,0:T(8,128)} %dinv_hbm.1), custom_call_target="tpu_custom_call" | custom-call | tf_op jit(solution)/shard_map/pallas_call | solution.py:340
  38.8 0.6 %copy.8 = f32[1,1,8,512]{3,2,1,0:T(8,128)} copy(f32[1,1,8,512]{3,2,1,0:T(8,128)S(1)} %bitcast.4) | data formatting | bytes 32768
  39.4 0.6 %copy.9 = f32[16,32]{1,0:T(8,128)} copy(f32[16,32]{1,0:T(8,128)S(1)} %get-tuple-element.7) | data formatting | bytes 4096

commit v7 on v6

--- a/solution.py
+++ b/solution.py
@@ -202,6 +202,8 @@
         for b in range(2):
             got(1, 0, b)
             pass_y(1, 0, b, 2 * b - 1)
+            got(1, 2 * b - 1, b)
+            pass_y(1, 2 * b - 1, b, 1 - 2 * b)
             for dy in (-1, 1):
                 got(2, dy, b)
                 pass_across(dy, b)
@@ -212,9 +214,6 @@
         for b in range(2):
             got(2, 0, b)
             pass_across(0, b)
-        for b in range(2):
-            got(1, 2 * b - 1, b)
-            pass_y(1, 2 * b - 1, b, 1 - 2 * b)
 
         for way in range(2):
             sign = 1 - 2 * way

time: 40.1 us -> 40.1 us (level)
  no operation moved by 1% of the time
where the time goes in v7:
time: 40.1 us; the launch traced here: 40 us
  Pallas kernels  38.1 us (95%)
  local copies, waits for them, and re-layouts  1.21 us (3%)
  between operations  0.64 us (2%)
    pallas_call x1, Pallas kernels, local(): pl.pallas_call(kernel, out_shape=(pltpu.VMEM((8, 512), F32), pltpu.VMEM((...  38.1 us
    unnamed x2, local copies, waits for them, and re-layouts  1.21 us

profile of v7, /device:TPU:1, one launch (start us, length us, event | category | flops | bytes accessed | tf_op | source)
XLA Modules:
  0.0 40.0 jit_solution(14790638345223699351)
XLA Ops:
  0.6 38.1 %shard_map.59 = (f32[8,512]{1,0:T(8,128)S(1)}, f32[16,32]{1,0:T(8,128)S(1)}) custom-call(f32[256,128]{1,0:T(8,128)} %bitcast.6, s32[1,2]{1,0:T(1,128)} %bitcast.7, f32[128,512]{1,0:T(8,128)} %bitcast.5, f32[16,32]{1,0:T(8,128)} %dinv_hbm.1), custom_call_target="tpu_custom_call" | custom-call | tf_op jit(solution)/shard_map/pallas_call | solution.py:339
  38.8 0.6 %copy.8 = f32[1,1,8,512]{3,2,1,0:T(8,128)} copy(f32[1,1,8,512]{3,2,1,0:T(8,128)S(1)} %bitcast.4) | data formatting | bytes 32768
  39.4 0.6 %copy.9 = f32[16,32]{1,0:T(8,128)} copy(f32[16,32]{1,0:T(8,128)S(1)} %get-tuple-element.7) | data formatting | bytes 4096
